TPU v7x, 256 devices: a whole 4x4x8 slice. The times are simulated.
256 devices in a mesh: leaf: 16 (over y, x), sep: 8 (over z), mode: 2 (over core).
Axes of the slice: x: 4, y: 4, z: 8, core: 2. Of those that a mesh axis runs over, the one named last changes fastest.
Arguments:
- modes: bfloat16 [1024, 2048, 256], P(('leaf', 'sep'), 'mode'), may hold values from -0.125 to 0.125
- coupling: bfloat16 [1024, 2048, 256], P(('leaf', 'sep'), 'mode'), may hold values from -6 to 6
- eigenvalues: float32 [1024, 256], P(('leaf', 'sep'), 'mode'), may hold values from 200 to 4000
- separator_of: int32 [1024, 1], P(('leaf', 'sep')), may hold values from 0 to 7; in each aligned block of 8 rows (0 to 7, 8 to 15, ...) at most 2 rows name the same one
- row_offset: int32 [1024], P(('leaf', 'sep')), may hold values from 0 to 256
- stiffness: bfloat16 [8, 512, 512], P('sep', None, ('leaf', 'mode')), may hold values from -1 to 40
- start_block: bfloat16 [8, 512, 256], P('sep', ('leaf', 'mode')), may hold values from -40 to 40
- rotations: bfloat16 [8, 2, 256, 256], P('sep'), may hold values from -0.375 to 0.375
Outputs:
- subspace: bfloat16 [8, 512, 256], P('sep', ('leaf', 'mode'))
- column_norms: float32 [8, 2, 256], P('sep')
Inputs may be any that keep to these rules, and one draw needn't show every extreme that they name: `separator_of`: among the 8 leaves of one device at most 2 couple to one separator, and in every draw some separator gets exactly 2 of them.
All inputs are finite; a program needn't handle non-finite values.
Results may differ from a plain program's by a relative error of at most 0.0075.
Values may be sent and summed in bfloat16 or wider, within the bound.
No kernel may reach another device: no remote copies, remote signals or barrier semaphores. Data moves between devices by JAX's collectives and lax.ppermute only.
A program may use at most 64 MiB of HBM per device.

v0:
```python
import jax
import jax.numpy as jnp
from jax import lax
from jax.sharding import PartitionSpec as P

SEP_ROWS = 512
CAP = 2
ITERS = 2
epsilon = 1e-06


def leaf_projection(modes, coupling, eigenvalues):
    summed = lax.psum_scatter(
        jnp.einsum("ldm,ldw->mlw", modes, coupling, preferred_element_type=jnp.float32),
        "mode",
        scatter_dimension=0,
        tiled=True,
    )
    return (summed / jnp.sqrt(eigenvalues.T)[:, :, None]).astype(jnp.bfloat16)


def route_blocks(scaled, separator_of, row_offset):
    groups = lax.axis_size("sep")
    leaves = scaled.shape[1]
    target = separator_of[:, 0]
    leaf_order = jnp.arange(leaves)
    earlier = (target[:, None] == target[None, :]) & (leaf_order[None, :] < leaf_order[:, None])
    position = jnp.sum(earlier.astype(jnp.int32), 1)
    slot_of = target * CAP + position
    slot_table = slot_of[None, :] == jnp.arange(groups * CAP)[:, None]
    send_blocks = jnp.einsum(
        "sl,mlw->smw", slot_table.astype(jnp.bfloat16), scaled, preferred_element_type=jnp.float32
    ).astype(jnp.bfloat16)
    send_offsets = jnp.sum(jnp.where(slot_table, row_offset[None, :], 0), 1)
    block_shape = (groups, CAP, send_blocks.shape[1], send_blocks.shape[2])
    got_blocks, got_offsets = (
        lax.all_to_all(
            send_blocks.reshape(block_shape), "sep", split_axis=0, concat_axis=0, tiled=True
        ),
        lax.all_to_all(
            send_offsets.reshape(groups, CAP), "sep", split_axis=0, concat_axis=0, tiled=True
        ),
    )
    return (
        got_blocks.reshape(groups * CAP, block_shape[2], block_shape[3]),
        got_offsets.reshape(groups * CAP),
    )


def coupled_correction(full_block, blocks, offsets):
    width_rows = blocks.shape[2]

    def add_slot(slot_index, accumulated):
        offset = offsets[slot_index]
        weights = blocks[slot_index]
        window = lax.dynamic_slice_in_dim(full_block, offset, width_rows, 0)
        projected = jnp.dot(weights, window, preferred_element_type=jnp.float32).astype(
            jnp.bfloat16
        )
        update = jnp.einsum("mw,mc->wc", weights, projected, preferred_element_type=jnp.float32)
        current = lax.dynamic_slice_in_dim(accumulated, offset, width_rows, 0)
        return lax.dynamic_update_slice_in_dim(accumulated, current + update, offset, 0)

    initial = jnp.zeros(full_block.shape, jnp.float32)
    return lax.fori_loop(0, blocks.shape[0], add_slot, initial)


def gather_rows(own_block):
    return lax.all_gather(own_block, ("leaf", "mode"), axis=0, tiled=True)


def per_device(
    modes, coupling, eigenvalues, separator_of, row_offset, stiffness, start_block, rotations
):
    scaled = leaf_projection(modes, coupling, eigenvalues)
    blocks, offsets = route_blocks(scaled, separator_of, row_offset)
    stiff_columns = stiffness[0]
    own_block = start_block[0]
    ritz_turns = rotations[0]
    own_rows = own_block.shape[0]
    norm_list = []
    for iteration in range(ITERS):
        full_block = gather_rows(own_block)
        correction = coupled_correction(full_block, blocks, offsets)

        def assemble_rows(first_row, row_count, block_now=own_block, correction_now=correction):
            product = jnp.dot(stiff_columns, block_now, preferred_element_type=jnp.float32)
            return product - correction_now

        summed = lax.psum_scatter(
            assemble_rows(jnp.int32(0), lax.axis_size(("leaf", "mode")) * own_rows),
            ("leaf", "mode"),
            scatter_dimension=0,
            tiled=True,
        )
        squares = lax.psum(jnp.sum(summed * summed, 0), ("leaf", "mode"))
        column_scale = jnp.sqrt(squares / SEP_ROWS + epsilon)
        normed = (summed / column_scale).astype(jnp.bfloat16)
        own_block = jnp.dot(
            normed, ritz_turns[iteration], preferred_element_type=jnp.float32
        ).astype(jnp.bfloat16)
        norm_list.append(column_scale)
    return (own_block[None], jnp.stack(norm_list)[None])


def solution(mesh):
    in_specs = (
        P(("leaf", "sep"), "mode", None),
        P(("leaf", "sep"), "mode", None),
        P(("leaf", "sep"), "mode"),
        P(("leaf", "sep"), None),
        P(("leaf", "sep")),
        P("sep", None, ("leaf", "mode")),
        P("sep", ("leaf", "mode"), None),
        P("sep", None, None, None),
    )
    out_specs = (P("sep", ("leaf", "mode"), None), P("sep", None, None))
    return jax.shard_map(
        per_device, mesh=mesh, in_specs=in_specs, out_specs=out_specs, check_vma=False
    )
```

profile of v0, /device:TPU:1, one launch (start us, length us, event | category | flops | bytes accessed | tf_op | source)
XLA Modules:
  0.0 560.8 jit_solution(13401757239637969915)
XLA Ops:
  7.3 6.2 %convolution_bitcast_fusion = f32[256,8,256]{0,2,1:T(8,128)} fusion(bf16[8,1024,256]{2,1,0:T(8,128)(2,1)} %param.13, bf16[8,1024,256]{2,1,0:T(8,128)(2,1)} %param.12), kind=kOutput, calls=%fused_computation.13 | convolution fusion | flops 1073741824 | bytes 10485760 | tf_op jit(solution)/shard_map/ldm,ldw->mlw/dot_general | solution.py:14
  14.5 9.0 %all-to-all-start = ((s32[8,1,2]{2,1,0:T(1,128)}), s32[8,1,2]{2,1,0:T(1,128)S(1)}, u32[]{:S(2)}, u32[]{:S(2)}) async-start(s32[8,1,2]{2,1,0:T(1,128)} %bitcast.7), calls=%async_computation | async-start | bytes 8192 | tf_op jit(solution)/shard_map/all_to_all | solution.py:40
  23.5 9.3 %reduce-scatter.6.cloned.1.call-done = f32[128,8,256]{0,2,1:T(8,128)} async-done(((f32[256,8,256]{0,2,1:T(8,128)}), f32[128,8,256]{0,2,1:T(8,128)}) %reduce-scatter.6.cloned.1.call-update) | async-done | bytes 1048592 | tf_op jit(solution)/shard_map/reduce_scatter | solution.py:13
  37.3 6.8 %all-to-all-start.1 = ((bf16[8,2,128,256]{3,1,2,0:T(2,128)(2,1)}), bf16[8,2,128,256]{3,1,2,0:T(2,128)(2,1)S(1)}, u32[]{:S(2)}, u32[]{:S(2)}) async-start(bf16[8,2,128,256]{3,1,2,0:T(2,128)(2,1)} %copy.30), calls=%async_computation.2 | async-start | bytes 2097152 | tf_op jit(solution)/shard_map/all_to_all | solution.py:37
  44.2 25.3 %all-gather = bf16[1,512,256]{2,1,0:T(8,128)(2,1)S(1)} all-gather(bf16[1,16,256]{2,1,0:T(8,128)(2,1)S(1)} %copy-done.1), channel_id=2, replica_groups=mesh['leaf'=16,'sep'=8,'mode'=2] {'leaf','mode'}, dimensions={1}, use_global_device_ids=true | all-gather | bytes 270336 | tf_op jit(solution)/shard_map/all_gather | solution.py:69
  70.8 2.6 all-to-all-done.1
  73.6 74.0 %while.26 = (s32[]{:T(128)}, f32[512,256]{1,0:T(8,128)S(1)}, s32[16]{0:T(128)S(1)}, bf16[16,128,256]{2,1,0:T(8,128)(2,1)S(1)}, bf16[512,256]{1,0:T(8,128)(2,1)S(1)}, /*index=5*/s32[]{:T(128)}, s32[]{:T(128)}, s32[]{:T(128)}) while((s32[]{:T(128)}, f32[512,256]{1,0:T(8,128)S(1)}, s32[16]{0:T(128)S(1)}, bf16[16,128,256]{2,1,0:T(8,128)(2,1)S(1)}, ...), condition=%wide.region_4.5_spmd, body=%wide.region_3.4_spmd.sunk | while | flops 33652740 | bytes 1312903 | solution.py:65
  148.8 80.6 %reduce-scatter.8.cloned.1.call-done = f32[16,256]{1,0:T(8,128)} async-done(((f32[512,256]{1,0:T(8,128)}), f32[16,256]{1,0:T(8,128)}) %reduce-scatter.8.cloned.1.call-update) | async-done | bytes 16400 | tf_op jit(solution)/shard_map/reduce_scatter | solution.py:90
  230.1 64.6 %psum.14 = f32[256]{0:T(256)S(1)} all-reduce(f32[256]{0:T(256)S(1)} %multiply_reduce_fusion.1), channel_id=1, replica_groups=mesh['leaf'=16,'sep'=8,'mode'=2] {'leaf','mode'}, use_global_device_ids=true, to_apply=%region_7.8 | all-reduce | flops 256 | bytes 2048 | tf_op jit(solution)/shard_map/psum | solution.py:96
  295.6 22.6 %all_gather.7 = bf16[512,256]{1,0:T(8,128)(2,1)S(1)} all-gather(bf16[16,256]{1,0:T(8,128)(2,1)S(1)} %convolution_convert_fusion.4), channel_id=1, replica_groups=mesh['leaf'=16,'sep'=8,'mode'=2] {'leaf','mode'}, dimensions={0}, use_global_device_ids=true | all-gather | bytes 270336 | tf_op jit(solution)/shard_map/all_gather | solution.py:69
  318.3 85.1 %while.27 = (s32[]{:T(128)}, f32[512,256]{0,1:T(8,128)S(1)}, s32[16]{0:T(128)S(1)}, bf16[16,128,256]{2,1,0:T(8,128)(2,1)S(1)}, bf16[512,256]{1,0:T(8,128)(2,1)S(1)}, /*index=5*/s32[]{:T(128)}, s32[]{:T(128)}, s32[]{:T(128)}) while((s32[]{:T(128)}, f32[512,256]{0,1:T(8,128)S(1)}, s32[16]{0:T(128)S(1)}, bf16[16,128,256]{2,1,0:T(8,128)(2,1)S(1)}, ...), condition=%wide.region_9.10_spmd, body=%wide.region_8.9_spmd.sunk | while | flops 33652740 | bytes 2884751 | solution.py:65
  326.8 1.9 dynamic_update_slice.17
  332.1 1.9 dynamic_update_slice.17
  337.4 1.9 dynamic_update_slice.17
  347.9 1.9 dynamic_update_slice.17
  353.1 2.2 dynamic_update_slice.17
  358.7 1.9 dynamic_update_slice.17
  369.2 1.9 dynamic_update_slice.17
  374.5 2.2 dynamic_update_slice.17
  390.6 1.9 dynamic_update_slice.17
  395.8 2.2 dynamic_update_slice.17
  401.4 1.9 dynamic_update_slice.17
  404.7 82.7 %reduce-scatter.10.cloned.1.call-done = f32[16,256]{1,0:T(8,128)} async-done(((f32[512,256]{1,0:T(8,128)}), f32[16,256]{1,0:T(8,128)}) %reduce-scatter.10.cloned.1.call-update) | async-done | bytes 16400
  488.2 64.6 %psum.15 = f32[256]{0:T(256)S(1)} all-reduce(f32[256]{0:T(256)S(1)} %multiply_reduce_fusion), channel_id=1, replica_groups=mesh['leaf'=16,'sep'=8,'mode'=2] {'leaf','mode'}, use_global_device_ids=true, to_apply=%region_12.13 | all-reduce | flops 256 | bytes 2048 | tf_op jit(solution)/shard_map/psum | solution.py:96
  (179 shorter events, 86.9 us)
Async XLA Ops:
  7.2 140.5 %copy-start = (bf16[1,512,16]{1,2,0:T(8,128)(2,1)S(1)}, bf16[1,512,16]{1,2,0:T(8,128)(2,1)}, u32[]{:S(2)}) copy-start(bf16[1,512,16]{1,2,0:T(8,128)(2,1)} %param.17) | copy-start | bytes 49156
  7.2 6.3 %copy-start.4 = (s32[8,1]{0,1:T(1,128)S(1)}, s32[8,1]{0,1:T(1,128)}, u32[]{:S(2)}) copy-start(s32[8,1]{0,1:T(1,128)} %param.15) | copy-start | bytes 100
  7.2 6.5 %copy-start.5 = (s32[8]{0:T(128)S(1)}, s32[8]{0:T(128)}, u32[]{:S(2)}) copy-start(s32[8]{0:T(128)} %param.16) | copy-start | bytes 100
  7.2 16.3 %copy-start.2 = (f32[8,128]{1,0:T(8,128)S(1)}, f32[8,128]{1,0:T(8,128)}, u32[]{:S(2)}) copy-start(f32[8,128]{1,0:T(8,128)} %param.14) | copy-start | bytes 12292
  7.2 25.6 %reduce-scatter.6.cloned.1.call-start = ((), (), s32[]{:S(2)}) async-start(), calls=%async_computation.5 | async-start | bytes 3145728 | tf_op jit(solution)/shard_map/reduce_scatter | solution.py:13
  14.5 22.9 %all-to-all-start = ((s32[8,1,2]{2,1,0:T(1,128)}), s32[8,1,2]{2,1,0:T(1,128)S(1)}, u32[]{:S(2)}, u32[]{:S(2)}) async-start(s32[8,1,2]{2,1,0:T(1,128)} %bitcast.7), calls=%async_computation | async-start | bytes 8192 | tf_op jit(solution)/shard_map/all_to_all | solution.py:40
  34.5 9.6 %copy-start.1 = (bf16[1,16,256]{2,1,0:T(8,128)(2,1)S(1)}, bf16[1,16,256]{2,1,0:T(8,128)(2,1)}, u32[]{:S(2)}) copy-start(bf16[1,16,256]{2,1,0:T(8,128)(2,1)} %param.18) | copy-start | bytes 24580
  37.3 36.0 %all-to-all-start.1 = ((bf16[8,2,128,256]{3,1,2,0:T(2,128)(2,1)}), bf16[8,2,128,256]{3,1,2,0:T(2,128)(2,1)S(1)}, u32[]{:S(2)}, u32[]{:S(2)}) async-start(bf16[8,2,128,256]{3,1,2,0:T(2,128)(2,1)} %copy.30), calls=%async_computation.2 | async-start | bytes 2097152 | tf_op jit(solution)/shard_map/all_to_all | solution.py:37
  44.1 185.3 %reduce-scatter.8.cloned.1.call-start = ((), (), s32[]{:S(2)}) async-start(), calls=%async_computation.6 | async-start | bytes 540672 | tf_op jit(solution)/shard_map/reduce_scatter | solution.py:90
  73.6 221.1 %copy-start.3 = (bf16[1,2,256,256]{3,2,1,0:T(8,128)(2,1)S(1)}, bf16[1,2,256,256]{3,2,1,0:T(8,128)(2,1)}, u32[]{:S(2)}) copy-start(bf16[1,2,256,256]{3,2,1,0:T(8,128)(2,1)} %param.19) | copy-start | bytes 786436
  148.7 338.6 %reduce-scatter.10.cloned.1.call-start = ((), (), s32[]{:S(2)}) async-start(), calls=%async_computation.7 | async-start | bytes 540672
Sparse Core Ops, SparseCore 0:
  13.6 19.1 reduce-scatter.5
  148.9 80.5 reduce-scatter.7
  404.8 82.4 reduce-scatter.9
where the time goes:
time: 562 us; the launch traced here: 561 us
  blocking collectives  177 us (31%)
  waiting for transfers between devices  175 us (31%)
  local copies, waits for them, and re-layouts  89.7 us (16%)
  loops' own time  63.5 us (11%)
  matrix products  21.7 us (4%)
  starting transfers between devices  15.9 us (3%)
  between operations  13.9 us (2%)
    psum x2, blocking collectives, per_device(): squares = lax.psum(jnp.sum(summed * summed, 0), ('leaf', 'mode'))  129 us
    unnamed x4, waiting for transfers between devices  82.7 us
    reduce_scatter x1, waiting for transfers between devices, per_device(): lax.psum_scatter(assemble_rows(jnp.int32(0), lax.axis_size(('leaf', 'mode...  80.6 us
    another operation x2, loops' own time, coupled_correction(): return lax.fori_loop(0, blocks.shape[0], add_slot, initial)  63.5 us
    dynamic_update_slice x48, local copies, waits for them, and re-layouts, add_slot(): lax.dynamic_update_slice_in_dim(accumulated, current + update, offset, 0)  60.6 us
    all_gather x2, blocking collectives, gather_rows(): return lax.all_gather(own_block, ('leaf', 'mode'), axis=0, tiled=True)  48 us
    dynamic_slice x32, local copies, waits for them, and re-layouts, add_slot(): offset = offsets[slot_index]  18.8 us
    dot_general x32, matrix products, add_slot(): jnp.einsum('mw,mc->wc', weights, projected, preferred_element_type=jnp.fl...  11.9 us
  transfers between devices with their start and end apart: 5, of which 4 were waited for; matrix products, arithmetic and copies ran while one was open for 1% of the time, Pallas kernels for 0%

commit v1 on v0

--- a/solution.py
+++ b/solution.py
@@ -7,6 +7,11 @@
 CAP = 2
 ITERS = 2
 epsilon = 1e-06
+
+
+def summed_here(x, mesh_axis):
+    parts = lax.all_gather(x, mesh_axis)
+    return jnp.sum(parts, axis=0)
 
 
 def leaf_projection(modes, coupling, eigenvalues):
@@ -93,7 +98,7 @@
             scatter_dimension=0,
             tiled=True,
         )
-        squares = lax.psum(jnp.sum(summed * summed, 0), ("leaf", "mode"))
+        squares = summed_here(jnp.sum(summed * summed, 0), ("leaf", "mode"))
         column_scale = jnp.sqrt(squares / SEP_ROWS + epsilon)
         normed = (summed / column_scale).astype(jnp.bfloat16)
         own_block = jnp.dot(

time: 562 us -> 484 us (0.86)
  blocking collectives: 177 us -> 99.9 us
    psum x2 -> x0, blocking collectives: 129 us -> none  [per_device(): squares = lax.psum(jnp.sum(summed * summed, 0), ('leaf', 'mode'))]
    all_gather x0 -> x2, blocking collectives: none -> 51.9 us  [summed_here(): parts = lax.all_gather(x, mesh_axis)]
where the time goes in v1:
time: 484 us; the launch traced here: 483 us
  waiting for transfers between devices  175 us (36%)
  blocking collectives  99.9 us (21%)
  local copies, waits for them, and re-layouts  89.7 us (19%)
  loops' own time  63.5 us (13%)
  matrix products  21.7 us (4%)
  starting transfers between devices  15.9 us (3%)
  between operations  13.9 us (3%)
    unnamed x4, waiting for transfers between devices  82 us
    reduce_scatter x1, waiting for transfers between devices, per_device(): lax.psum_scatter(assemble_rows(jnp.int32(0), lax.axis_size(('leaf', 'mode...  80.6 us
    another operation x2, loops' own time, coupled_correction(): return lax.fori_loop(0, blocks.shape[0], add_slot, initial)  63.5 us
    dynamic_update_slice x48, local copies, waits for them, and re-layouts, add_slot(): lax.dynamic_update_slice_in_dim(accumulated, current + update, offset, 0)  60.6 us
    all_gather x2, blocking collectives, summed_here(): parts = lax.all_gather(x, mesh_axis)  51.9 us
    all_gather x2, blocking collectives, gather_rows(): return lax.all_gather(own_block, ('leaf', 'mode'), axis=0, tiled=True)  48 us
    dynamic_slice x32, local copies, waits for them, and re-layouts, add_slot(): offset = offsets[slot_index]  18.8 us
    dot_general x32, matrix products, add_slot(): jnp.einsum('mw,mc->wc', weights, projected, preferred_element_type=jnp.fl...  11.9 us
  transfers between devices with their start and end apart: 5, of which 4 were waited for; matrix products, arithmetic and copies ran while one was open for 1% of the time, Pallas kernels for 0%

profile of v1, /device:TPU:1, one launch (start us, length us, event | category | flops | bytes accessed | tf_op | source)
XLA Modules:
  0.0 483.0 jit_solution(13514919044863120218)
XLA Ops:
  7.3 6.2 %convolution_bitcast_fusion = f32[256,8,256]{0,2,1:T(8,128)} fusion(bf16[8,1024,256]{2,1,0:T(8,128)(2,1)} %param.13, bf16[8,1024,256]{2,1,0:T(8,128)(2,1)} %param.12), kind=kOutput, calls=%fused_computation.13 | convolution fusion | flops 1073741824 | bytes 10485760 | tf_op jit(solution)/shard_map/ldm,ldw->mlw/dot_general | solution.py:19
  14.5 9.0 %all-to-all-start = ((s32[8,1,2]{2,1,0:T(1,128)}), s32[8,1,2]{2,1,0:T(1,128)S(1)}, u32[]{:S(2)}, u32[]{:S(2)}) async-start(s32[8,1,2]{2,1,0:T(1,128)} %bitcast.7), calls=%async_computation | async-start | bytes 8192 | tf_op jit(solution)/shard_map/all_to_all | solution.py:45
  23.5 9.3 %reduce-scatter.6.cloned.1.call-done = f32[128,8,256]{0,2,1:T(8,128)} async-done(((f32[256,8,256]{0,2,1:T(8,128)}), f32[128,8,256]{0,2,1:T(8,128)}) %reduce-scatter.6.cloned.1.call-update) | async-done | bytes 1048592 | tf_op jit(solution)/shard_map/reduce_scatter | solution.py:18
  37.3 6.8 %all-to-all-start.1 = ((bf16[8,2,128,256]{3,1,2,0:T(2,128)(2,1)}), bf16[8,2,128,256]{3,1,2,0:T(2,128)(2,1)S(1)}, u32[]{:S(2)}, u32[]{:S(2)}) async-start(bf16[8,2,128,256]{3,1,2,0:T(2,128)(2,1)} %copy.30), calls=%async_computation.2 | async-start | bytes 2097152 | tf_op jit(solution)/shard_map/all_to_all | solution.py:42
  44.2 25.3 %all-gather = bf16[1,512,256]{2,1,0:T(8,128)(2,1)S(1)} all-gather(bf16[1,16,256]{2,1,0:T(8,128)(2,1)S(1)} %copy-done.1), channel_id=2, replica_groups=mesh['leaf'=16,'sep'=8,'mode'=2] {'leaf','mode'}, dimensions={1}, use_global_device_ids=true | all-gather | bytes 270336 | tf_op jit(solution)/shard_map/all_gather | solution.py:74
  70.8 2.6 all-to-all-done.1
  73.6 74.0 %while.26 = (s32[]{:T(128)}, f32[512,256]{1,0:T(8,128)S(1)}, s32[16]{0:T(128)S(1)}, bf16[16,128,256]{2,1,0:T(8,128)(2,1)S(1)}, bf16[512,256]{1,0:T(8,128)(2,1)S(1)}, /*index=5*/s32[]{:T(128)}, s32[]{:T(128)}, s32[]{:T(128)}) while((s32[]{:T(128)}, f32[512,256]{1,0:T(8,128)S(1)}, s32[16]{0:T(128)S(1)}, bf16[16,128,256]{2,1,0:T(8,128)(2,1)S(1)}, ...), condition=%wide.region_4.5_spmd, body=%wide.region_3.4_spmd.sunk | while | flops 33652740 | bytes 1312903 | solution.py:70
  148.8 80.6 %reduce-scatter.8.cloned.1.call-done = f32[16,256]{1,0:T(8,128)} async-done(((f32[512,256]{1,0:T(8,128)}), f32[16,256]{1,0:T(8,128)}) %reduce-scatter.8.cloned.1.call-update) | async-done | bytes 16400 | tf_op jit(solution)/shard_map/reduce_scatter | solution.py:95
  230.1 25.9 %all-gather.3 = f32[32,1,256]{2,1,0:T(1,128)S(1)} all-gather(f32[1,1,256]{2,1,0:T(1,128)S(1)} %bitcast.70), channel_id=3, replica_groups=mesh['leaf'=16,'sep'=8,'mode'=2] {'leaf','mode'}, dimensions={0}, use_global_device_ids=true | all-gather | bytes 33792 | tf_op jit(solution)/shard_map/all_gather | solution.py:13
  257.0 22.7 %all_gather.21 = bf16[512,256]{1,0:T(8,128)(2,1)S(1)} all-gather(bf16[16,256]{1,0:T(8,128)(2,1)S(1)} %convolution_convert_fusion.4), channel_id=1, replica_groups=mesh['leaf'=16,'sep'=8,'mode'=2] {'leaf','mode'}, dimensions={0}, use_global_device_ids=true | all-gather | bytes 270336 | tf_op jit(solution)/shard_map/all_gather | solution.py:74
  279.7 85.1 %while.27 = (s32[]{:T(128)}, f32[512,256]{0,1:T(8,128)S(1)}, s32[16]{0:T(128)S(1)}, bf16[16,128,256]{2,1,0:T(8,128)(2,1)S(1)}, bf16[512,256]{1,0:T(8,128)(2,1)S(1)}, /*index=5*/s32[]{:T(128)}, s32[]{:T(128)}, s32[]{:T(128)}) while((s32[]{:T(128)}, f32[512,256]{0,1:T(8,128)S(1)}, s32[16]{0:T(128)S(1)}, bf16[16,128,256]{2,1,0:T(8,128)(2,1)S(1)}, ...), condition=%wide.region_9.10_spmd, body=%wide.region_8.9_spmd.sunk | while | flops 33652740 | bytes 2884751 | solution.py:70
  288.3 1.9 dynamic_update_slice.17
  293.6 1.9 dynamic_update_slice.17
  298.8 1.9 dynamic_update_slice.17
  309.3 1.9 dynamic_update_slice.17
  314.6 2.2 dynamic_update_slice.17
  320.2 1.9 dynamic_update_slice.17
  330.7 1.9 dynamic_update_slice.17
  335.9 2.2 dynamic_update_slice.17
  341.5 1.9 dynamic_update_slice.17
  352.0 1.9 dynamic_update_slice.17
  357.3 2.2 dynamic_update_slice.17
  366.1 81.9 %reduce-scatter.10.cloned.1.call-done = f32[16,256]{1,0:T(8,128)} async-done(((f32[512,256]{1,0:T(8,128)}), f32[16,256]{1,0:T(8,128)}) %reduce-scatter.10.cloned.1.call-update) | async-done | bytes 16400
  449.0 25.9 %all-gather.4 = f32[32,1,256]{2,1,0:T(1,128)S(1)} all-gather(f32[1,1,256]{2,1,0:T(1,128)S(1)} %bitcast.69), channel_id=4, replica_groups=mesh['leaf'=16,'sep'=8,'mode'=2] {'leaf','mode'}, dimensions={0}, use_global_device_ids=true | all-gather | bytes 33792 | tf_op jit(solution)/shard_map/all_gather | solution.py:13
  (181 shorter events, 87.0 us)
Async XLA Ops:
  7.2 140.5 %copy-start = (bf16[1,512,16]{1,2,0:T(8,128)(2,1)S(1)}, bf16[1,512,16]{1,2,0:T(8,128)(2,1)}, u32[]{:S(2)}) copy-start(bf16[1,512,16]{1,2,0:T(8,128)(2,1)} %param.17) | copy-start | bytes 49156
  7.2 6.3 %copy-start.4 = (s32[8,1]{0,1:T(1,128)S(1)}, s32[8,1]{0,1:T(1,128)}, u32[]{:S(2)}) copy-start(s32[8,1]{0,1:T(1,128)} %param.15) | copy-start | bytes 100
  7.2 6.5 %copy-start.5 = (s32[8]{0:T(128)S(1)}, s32[8]{0:T(128)}, u32[]{:S(2)}) copy-start(s32[8]{0:T(128)} %param.16) | copy-start | bytes 100
  7.2 16.3 %copy-start.2 = (f32[8,128]{1,0:T(8,128)S(1)}, f32[8,128]{1,0:T(8,128)}, u32[]{:S(2)}) copy-start(f32[8,128]{1,0:T(8,128)} %param.14) | copy-start | bytes 12292
  7.2 25.6 %reduce-scatter.6.cloned.1.call-start = ((), (), s32[]{:S(2)}) async-start(), calls=%async_computation.5 | async-start | bytes 3145728 | tf_op jit(solution)/shard_map/reduce_scatter | solution.py:18
  14.5 22.9 %all-to-all-start = ((s32[8,1,2]{2,1,0:T(1,128)}), s32[8,1,2]{2,1,0:T(1,128)S(1)}, u32[]{:S(2)}, u32[]{:S(2)}) async-start(s32[8,1,2]{2,1,0:T(1,128)} %bitcast.7), calls=%async_computation | async-start | bytes 8192 | tf_op jit(solution)/shard_map/all_to_all | solution.py:45
  34.5 9.6 %copy-start.1 = (bf16[1,16,256]{2,1,0:T(8,128)(2,1)S(1)}, bf16[1,16,256]{2,1,0:T(8,128)(2,1)}, u32[]{:S(2)}) copy-start(bf16[1,16,256]{2,1,0:T(8,128)(2,1)} %param.18) | copy-start | bytes 24580
  37.3 36.0 %all-to-all-start.1 = ((bf16[8,2,128,256]{3,1,2,0:T(2,128)(2,1)}), bf16[8,2,128,256]{3,1,2,0:T(2,128)(2,1)S(1)}, u32[]{:S(2)}, u32[]{:S(2)}) async-start(bf16[8,2,128,256]{3,1,2,0:T(2,128)(2,1)} %copy.30), calls=%async_computation.2 | async-start | bytes 2097152 | tf_op jit(solution)/shard_map/all_to_all | solution.py:42
  44.1 185.3 %reduce-scatter.8.cloned.1.call-start = ((), (), s32[]{:S(2)}) async-start(), calls=%async_computation.6 | async-start | bytes 540672 | tf_op jit(solution)/shard_map/reduce_scatter | solution.py:95
  73.6 182.6 %copy-start.3 = (bf16[1,2,256,256]{3,2,1,0:T(8,128)(2,1)S(1)}, bf16[1,2,256,256]{3,2,1,0:T(8,128)(2,1)}, u32[]{:S(2)}) copy-start(bf16[1,2,256,256]{3,2,1,0:T(8,128)(2,1)} %param.19) | copy-start | bytes 786436
  148.7 299.3 %reduce-scatter.10.cloned.1.call-start = ((), (), s32[]{:S(2)}) async-start(), calls=%async_computation.7 | async-start | bytes 540672
Sparse Core Ops, SparseCore 0:
  13.6 19.1 reduce-scatter.5
  148.9 80.5 reduce-scatter.7
  366.2 81.7 reduce-scatter.9
